TPU v7x, 32 devices: a whole 2x2x4 slice. The times are simulated.
32 devices in a mesh: seq: 4 (over z), dp: 8 (over y, x, core).
Axes of the slice: x: 2, y: 2, z: 4, core: 2. Of those that a mesh axis runs over, the one named last changes fastest.
Arguments:
- hidden_in: bfloat16 [16, 2048, 1024], P('dp', 'seq'), may hold values from -6 to 6
- mixer_weights: float32 [1, 5, 1024, 1024], P(None, None, 'dp'), may hold values from -0.1875 to 0.1875
- channel_in_weights: float32 [1, 2, 1024, 2816], P(None, None, 'dp'), may hold values from -0.1875 to 0.1875
- channel_out_weights: float32 [1, 2816, 1024], P(None, 'dp'), may hold values from -0.109375 to 0.109375
- decay_rates: float32 [1, 8], replicated, may hold values from 0 to 0.034, as said below
- doc_lengths: int32 [16, 4], P('dp'), may hold values from 1 to 1024, 2048 in all within a row
- out_cotangent: bfloat16 [16, 2048, 1024], P('dp', 'seq'), may hold values from -6 to 6
Outputs:
- block_output: bfloat16 [16, 2048, 1024], P('dp', 'seq')
- input_gradient: float32 [16, 2048, 1024], P('dp', 'seq')
- mixer_gradient: float32 [1, 5, 1024, 1024], P(None, None, 'dp')
- channel_in_gradient: float32 [1, 2, 1024, 2816], P(None, None, 'dp')
- channel_out_gradient: float32 [1, 2816, 1024], P(None, 'dp')
Inputs may be any that keep to these rules, and one draw needn't show every extreme that they name: `decay_rates`: positive decay rates. `doc_lengths`: each row's 4 lengths add up to 2048.
All inputs are finite; a program needn't handle non-finite values.
Results may differ from a plain program's by a relative error of at most 0.02.
Values may be sent and summed in bfloat16 or wider, within the bound.
No kernel may reach another device: no remote copies, remote signals or barrier semaphores. Data moves between devices by JAX's collectives and lax.ppermute only.
A program may use at most 256 MiB of HBM per device.

v0:
```python
import jax
import jax.numpy as jnp
from jax import lax
from jax.sharding import PartitionSpec as P

EPS = 1e-06
FULL_PRECISION = lax.Precision.HIGHEST


def passed_along(value, axis, steps):
    count = lax.axis_size(axis)
    leading, last = (max(0, -steps), min(count, count - steps))
    return lax.ppermute(value, axis, [(source, source + steps) for source in range(leading, last)])


def product(left, right):
    return jnp.dot(left, right, preferred_element_type=jnp.float32)


def rms_norm(value_rows):
    factor = lax.rsqrt(jnp.mean(value_rows * value_rows, axis=-1, keepdims=True) + EPS)
    return (value_rows * factor, factor)


def norm_back(value_rows, factor, upstream):
    features = value_rows.shape[-1]
    inner_sum = jnp.sum(upstream * value_rows, axis=-1, keepdims=True)
    return factor * upstream - factor * factor * factor / features * value_rows * inner_sum


def swish_slope(value_rows):
    sigmoid_part = jax.nn.sigmoid(value_rows)
    return sigmoid_part * (1.0 + value_rows * (1.0 - sigmoid_part))


def doc_index(doc_ends, places):
    compare = places[None, :, None] >= doc_ends[:, None, :]
    return jnp.sum(compare.astype(jnp.int32), axis=-1, dtype=jnp.int32)


def decay_tables(rates, doc_ends, start, count):
    float_kind = rates.dtype
    offsets = jnp.arange(count, dtype=jnp.int32)
    start = jnp.asarray(start, dtype=jnp.int32)
    doc_here = doc_index(doc_ends, start + offsets)
    before_place = jnp.full((1,), -1, dtype=jnp.int32) + start
    doc_before = doc_index(doc_ends, before_place)[:, 0]
    doc_last = doc_here[:, count - 1]
    distance = jnp.maximum(offsets[:, None] - offsets[None, :], 0).astype(float_kind)
    causal = offsets[:, None] >= offsets[None, :]
    linked = causal[None] & (doc_here[:, :, None] == doc_here[:, None, :])
    intra_vals = jnp.exp(-rates[None, :, None, None] * distance[None, None])
    intra = jnp.where(linked[:, None], intra_vals, jnp.zeros_like(intra_vals))
    ahead = (offsets + 1).astype(float_kind)
    behind = (count - 1 - offsets).astype(float_kind)
    entry_vals = jnp.exp(-rates[None, None, :] * ahead[None, :, None])
    entry = jnp.where(
        (doc_here == doc_before[:, None])[:, :, None], entry_vals, jnp.zeros_like(entry_vals)
    )
    leaving_vals = jnp.exp(-rates[None, None, :] * behind[None, :, None])
    leaving = jnp.where(
        (doc_here == doc_last[:, None])[:, :, None], leaving_vals, jnp.zeros_like(leaving_vals)
    )
    length_value = jnp.asarray(count, dtype=float_kind)
    passing_vals = jnp.exp(-rates * length_value)[None, :] + jnp.zeros(
        (doc_last.shape[0], 1), float_kind
    )
    passing = jnp.where(
        (doc_last == doc_before)[:, None], passing_vals, jnp.zeros_like(passing_vals)
    )
    return (intra, entry, leaving, passing)


def block_out(per_head_queries, per_head_keys, per_head_values, tables, state_in):
    scores = (
        jnp.einsum("rthd,rshd->rhts", per_head_queries, per_head_keys, precision=FULL_PRECISION)
        * tables[0]
    )
    local_part = jnp.einsum("rhts,rshe->rthe", scores, per_head_values, precision=FULL_PRECISION)
    carried = (
        jnp.einsum("rthd,rhde->rthe", per_head_queries, state_in, precision=FULL_PRECISION)
        * tables[1][..., None]
    )
    return local_part + carried


def block_state(per_head_keys, per_head_values, tables):
    return jnp.einsum(
        "rshd,rshe->rhde",
        per_head_keys * tables[2][..., None],
        per_head_values,
        precision=FULL_PRECISION,
    )


def block_back(
    per_head_queries, per_head_keys, per_head_values, upstream, tables, state_in, state_grad
):
    intra, entry, leaving, passing = tables
    scores = (
        jnp.einsum("rthd,rshd->rhts", per_head_queries, per_head_keys, precision=FULL_PRECISION)
        * intra
    )
    score_grad = (
        jnp.einsum("rthe,rshe->rhts", upstream, per_head_values, precision=FULL_PRECISION) * intra
    )
    query_grad = jnp.einsum("rhts,rshd->rthd", score_grad, per_head_keys, precision=FULL_PRECISION)
    query_grad = (
        query_grad
        + jnp.einsum("rthe,rhde->rthd", upstream, state_in, precision=FULL_PRECISION)
        * entry[..., None]
    )
    key_grad = jnp.einsum("rhts,rthd->rshd", score_grad, per_head_queries, precision=FULL_PRECISION)
    key_grad = (
        key_grad
        + jnp.einsum("rshe,rhde->rshd", per_head_values, state_grad, precision=FULL_PRECISION)
        * leaving[..., None]
    )
    value_grad = jnp.einsum("rhts,rthe->rshe", scores, upstream, precision=FULL_PRECISION)
    value_grad = (
        value_grad
        + jnp.einsum("rshd,rhde->rshe", per_head_keys, state_grad, precision=FULL_PRECISION)
        * leaving[..., None]
    )
    return (query_grad, key_grad, value_grad)


def carry_forward(passing, local_state):

    def step_forward(turn_index, incoming):
        outgoing = passing[..., None, None] * incoming + local_state
        return passed_along(outgoing.astype(jnp.bfloat16), "seq", 1).astype(outgoing.dtype)

    return lax.fori_loop(0, lax.axis_size("seq") - 1, step_forward, jnp.zeros_like(local_state))


def carry_backward(passing, local_grad):

    def retreat(turn_index, incoming):
        outgoing = passing[..., None, None] * incoming + local_grad
        return passed_along(outgoing.astype(jnp.bfloat16), "seq", -1).astype(outgoing.dtype)

    return lax.fori_loop(0, lax.axis_size("seq") - 1, retreat, jnp.zeros_like(local_grad))


def reduce_grads(terms):
    pieces = (
        lax.psum_scatter(
            terms[0].astype(jnp.bfloat16), "dp", scatter_dimension=1, tiled=True
        ).astype(jnp.float32),
        lax.psum_scatter(
            terms[1].astype(jnp.bfloat16), "dp", scatter_dimension=0, tiled=True
        ).astype(jnp.float32),
        lax.psum_scatter(
            terms[2].astype(jnp.bfloat16), "dp", scatter_dimension=1, tiled=True
        ).astype(jnp.float32),
        lax.psum_scatter(
            terms[3].astype(jnp.bfloat16), "dp", scatter_dimension=0, tiled=True
        ).astype(jnp.float32),
    )
    return (
        lax.psum(pieces[0].astype(jnp.bfloat16), "seq").astype(jnp.float32),
        lax.psum(pieces[1].astype(jnp.bfloat16), "seq").astype(jnp.float32),
        lax.psum(pieces[2].astype(jnp.bfloat16), "seq").astype(jnp.float32),
        lax.psum(pieces[3].astype(jnp.bfloat16), "seq").astype(jnp.float32),
    )


def local(
    hidden_in,
    mixer_weights,
    channel_in_weights,
    channel_out_weights,
    decay_rates,
    doc_lengths,
    out_cotangent,
):
    rows, tokens, features = hidden_in.shape
    layers = mixer_weights.shape[0]
    heads = decay_rates.shape[1]
    head_dim = features // heads
    count = rows * tokens
    head_shape = (rows, tokens, heads, head_dim)
    start = lax.axis_index("seq") * jnp.asarray(tokens, dtype=jnp.int32)
    doc_ends = jnp.cumsum(doc_lengths, axis=1, dtype=jnp.int32)
    resid = hidden_in.astype(jnp.float32).reshape(count, features)
    layer_index = 0
    gathered = (
        mixer_weights[layer_index].astype(jnp.bfloat16),
        channel_in_weights[layer_index].astype(jnp.bfloat16),
        channel_out_weights[layer_index].astype(jnp.bfloat16),
    )
    mixer_full = lax.all_gather(gathered[0], "dp", axis=1, tiled=True)
    channel_full = lax.all_gather(gathered[1], "dp", axis=1, tiled=True)
    down_full = lax.all_gather(gathered[2], "dp", axis=0, tiled=True)
    normed, factor_in = rms_norm(resid)
    normed_low = normed.astype(jnp.bfloat16)
    projected = jnp.einsum(
        "nd,kde->kne", normed_low, mixer_full[:4], preferred_element_type=jnp.float32
    )
    query_pre = projected[0]
    key_pre = projected[1]
    value_pre = projected[2]
    gate_pre = projected[3]
    per_head_queries = (query_pre * jax.nn.sigmoid(query_pre)).reshape(head_shape)
    per_head_keys = (key_pre * jax.nn.sigmoid(key_pre)).reshape(head_shape)
    per_head_values = value_pre.reshape(head_shape)
    tables = decay_tables(decay_rates[layer_index], doc_ends, start, tokens)
    local_state = block_state(per_head_keys, per_head_values, tables)
    state_in = carry_forward(tables[3], local_state)
    mixed = block_out(per_head_queries, per_head_keys, per_head_values, tables, state_in).reshape(
        count, features
    )
    mixed_norm, factor_mix = rms_norm(mixed)
    gated = (mixed_norm * gate_pre).astype(jnp.bfloat16)
    after_mixer = resid + product(gated, mixer_full[4])
    normed_two, factor_two = rms_norm(after_mixer)
    normed_two_low = normed_two.astype(jnp.bfloat16)
    pair = jnp.einsum(
        "nd,kdf->knf", normed_two_low, channel_full, preferred_element_type=jnp.float32
    )
    glu = (pair[0] * pair[1]).astype(jnp.bfloat16)
    saved = [
        (
            mixer_full,
            channel_full,
            down_full,
            resid,
            factor_in,
            normed_low,
            query_pre,
            key_pre,
            gate_pre,
            per_head_queries,
            per_head_keys,
            per_head_values,
            tables,
            state_in,
            mixed,
            mixed_norm,
            factor_mix,
            gated,
            after_mixer,
            factor_two,
            normed_two_low,
            pair,
            glu,
        )
    ]
    resid = after_mixer + product(glu, down_full)
    block_output = resid.astype(jnp.bfloat16).reshape(rows, tokens, features)
    upstream = out_cotangent.astype(jnp.float32).reshape(count, features)
    mixer_list = []
    channel_list = []
    down_list = []
    for layer_index in reversed(range(layers)):
        (
            mixer_full,
            channel_full,
            down_full,
            resid_in,
            factor_in,
            normed_low,
            query_pre,
            key_pre,
            gate_pre,
            per_head_queries,
            per_head_keys,
            per_head_values,
            tables,
            state_in,
            mixed,
            mixed_norm,
            factor_mix,
            gated,
            after_mixer,
            factor_two,
            normed_two_low,
            pair,
            glu,
        ) = saved[layer_index]
        branch_low = upstream.astype(jnp.bfloat16)
        down_term = jnp.einsum("nf,nd->fd", glu, branch_low, preferred_element_type=jnp.float32)
        glu_grad = (
            jnp.einsum("nd,fd->nf", branch_low, down_full, preferred_element_type=jnp.float32)
            .astype(jnp.bfloat16)
            .astype(jnp.float32)
        )
        pair_grad = jnp.stack([glu_grad * pair[1], glu_grad * pair[0]]).astype(jnp.bfloat16)
        channel_term = jnp.einsum(
            "nd,knf->kdf", normed_two_low, pair_grad, preferred_element_type=jnp.float32
        )
        two_grad = jnp.einsum(
            "knf,kdf->nd", pair_grad, channel_full, preferred_element_type=jnp.float32
        )
        upstream_mid = upstream + norm_back(after_mixer, factor_two, two_grad)
        mixer_low = upstream_mid.astype(jnp.bfloat16)
        out_term = jnp.einsum("nd,ne->de", gated, mixer_low, preferred_element_type=jnp.float32)
        gated_grad = (
            jnp.einsum("ne,de->nd", mixer_low, mixer_full[4], preferred_element_type=jnp.float32)
            .astype(jnp.bfloat16)
            .astype(jnp.float32)
        )
        gate_grad = gated_grad * mixed_norm
        mixed_grad = norm_back(mixed, factor_mix, gated_grad * gate_pre).reshape(head_shape)
        local_grad = jnp.einsum(
            "rthd,rthe->rhde",
            per_head_queries * tables[1][..., None],
            mixed_grad,
            precision=FULL_PRECISION,
        )
        state_grad = carry_backward(tables[3], local_grad)
        query_grad, key_grad, value_grad = block_back(
            per_head_queries,
            per_head_keys,
            per_head_values,
            mixed_grad,
            tables,
            state_in,
            state_grad,
        )
        proj_grad = jnp.stack(
            [
                query_grad.reshape(count, features) * swish_slope(query_pre),
                key_grad.reshape(count, features) * swish_slope(key_pre),
                value_grad.reshape(count, features),
                gate_grad,
            ]
        ).astype(jnp.bfloat16)
        four_term = jnp.einsum(
            "nd,kne->kde", normed_low, proj_grad, preferred_element_type=jnp.float32
        )
        one_grad = jnp.einsum(
            "kne,kde->nd", proj_grad, mixer_full[:4], preferred_element_type=jnp.float32
        )
        upstream = upstream_mid + norm_back(resid_in, factor_in, one_grad)
        summed = reduce_grads((four_term, out_term, channel_term, down_term))
        mixer_list.append(jnp.concatenate([summed[0], summed[1][None]], axis=0))
        channel_list.append(summed[2])
        down_list.append(summed[3])
    mixer_gradient = jnp.stack(mixer_list[::-1])
    channel_in_gradient = jnp.stack(channel_list[::-1])
    channel_out_gradient = jnp.stack(down_list[::-1])
    input_gradient = upstream.reshape(rows, tokens, features)
    return (block_output, input_gradient, mixer_gradient, channel_in_gradient, channel_out_gradient)


def solution(mesh):
    in_specs = (
        P("dp", "seq", None),
        P(None, None, "dp", None),
        P(None, None, "dp", None),
        P(None, "dp", None),
        P(),
        P("dp", None),
        P("dp", "seq", None),
    )
    out_specs = (
        P("dp", "seq", None),
        P("dp", "seq", None),
        P(None, None, "dp", None),
        P(None, None, "dp", None),
        P(None, "dp", None),
    )
    return jax.shard_map(local, mesh=mesh, in_specs=in_specs, out_specs=out_specs, check_vma=False)
```

profile of v0, /device:TPU:0, one launch (start us, length us, event | category | flops | bytes accessed | tf_op | source)
XLA Modules:
  0.0 966.9 jit_solution(12912789637610193381)
XLA Ops:
  10.1 3.2 convert_element_type.150
  20.7 5.8 multiply_exponential_fusion
  26.6 51.9 %all-gather.7.cloned.1.call-done = bf16[1,5,1024,1024]{2,3,1,0:T(8,128)(2,1)} async-done(((bf16[1,5,128,1024]{2,3,1,0:T(8,128)(2,1)}), bf16[1,5,1024,1024]{2,3,1,0:T(8,128)(2,1)}) %all-gather.7.cloned.1.call-update) | async-done | bytes 10485776 | tf_op jit(solution)/shard_map/all_gather | solution.py:193
  78.5 16.3 %convolution_bitcast_fusion = f32[4,1024,1024]{1,2,0:T(8,128)} fusion(bf16[1,5,1024,1024]{2,3,1,0:T(8,128)(2,1)} %all-gather.7.cloned.1.call-done, bf16[1024,1024]{1,0:T(8,128)(2,1)} %fusion.65), kind=kOutput, calls=%fused_computation.30 | convolution fusion | flops 8589934592 | bytes 27262976 | tf_op jit(solution)/shard_map/nd,kde->kne/dot_general | solution.py:198
  94.7 10.2 %fusion.120 = (f32[1,1024,1024]{1,2,0:T(8,128)}, f32[1,1024,1024]{1,2,0:T(8,128)}, f32[1,1024,1024]{1,2,0:T(8,128)}) fusion(f32[4,1024,1024]{1,2,0:T(8,128)} %convolution_bitcast_fusion), kind=kLoop, calls=%fused_computation.166 | loop fusion | bytes 25165824 | tf_op jit(solution)/shard_map/slice | solution.py:201
  104.9 6.6 reshape_squeeze.3
  111.5 7.4 copy.119
  118.9 6.6 squeeze.13
  125.5 6.8 squeeze.12
  132.2 8.6 fusion.69
  140.8 48.7 %while.22 = (s32[]{:T(128)}, f32[2,8,128,128]{3,2,1,0:T(8,128)S(1)}, f32[2,8,128,128]{3,2,1,0:T(8,128)S(1)}, f32[8]{0:T(128)S(1)}, pred[2]{0:T(512)(128)(4,1)S(1)}, /*index=5*/s32[]{:T(128)}, s32[]{:T(128)}) while((s32[]{:T(128)}, f32[2,8,128,128]{3,2,1,0:T(8,128)S(1)}, f32[2,8,128,128]{3,2,1,0:T(8,128)S(1)}, f32[8]{0:T(128)S(1)}, ...), condition=%wide.region_5.6_spmd.clone, body=%wide.region_4.5_spmd.clone.sunk | while | flops 1310739 | bytes 6291745 | solution.py:134
  141.9 3.4 collective-permute-start
  145.3 11.9 %collective-permute-done = bf16[2,8,128,128]{3,2,1,0:T(8,128)(2,1)S(1)} collective-permute-done((bf16[2,8,128,128]{3,2,1,0:T(8,128)(2,1)}, bf16[2,8,128,128]{3,2,1,0:T(8,128)(2,1)S(1)}, u32[]{:S(2)}, u32[]{:S(2)}) %collective-permute-start) | collective-permute-done | bytes 524320 | tf_op jit(solution)/shard_map/while/body/eval_jaxpr/ppermute | solution.py:13
  158.4 4.3 collective-permute-start
  162.7 11.1 %collective-permute-done = bf16[2,8,128,128]{3,2,1,0:T(8,128)(2,1)S(1)} collective-permute-done((bf16[2,8,128,128]{3,2,1,0:T(8,128)(2,1)}, bf16[2,8,128,128]{3,2,1,0:T(8,128)(2,1)S(1)}, u32[]{:S(2)}, u32[]{:S(2)}) %collective-permute-start) | collective-permute-done | bytes 524320 | tf_op jit(solution)/shard_map/while/body/eval_jaxpr/ppermute | solution.py:13
  174.9 4.3 collective-permute-start
  179.2 10.1 %collective-permute-done = bf16[2,8,128,128]{3,2,1,0:T(8,128)(2,1)S(1)} collective-permute-done((bf16[2,8,128,128]{3,2,1,0:T(8,128)(2,1)}, bf16[2,8,128,128]{3,2,1,0:T(8,128)(2,1)S(1)}, u32[]{:S(2)}, u32[]{:S(2)}) %collective-permute-start) | collective-permute-done | bytes 524320 | tf_op jit(solution)/shard_map/while/body/eval_jaxpr/ppermute | solution.py:13
  189.6 9.2 fusion.119
  198.8 17.2 %fusion.118 = f32[2,8,512,512]{3,2,1,0:T(8,128)} fusion(f32[2,512,8,128]{1,0,3,2:T(2,128)S(1)} %copy-done.14, f32[2,512,8,128]{1,0,3,2:T(2,128)S(1)} %copy-done.13), kind=kOutput, calls=%fused_computation.164 | convolution fusion | flops 6450839552 | bytes 25165824 | tf_op jit(solution)/shard_map/rthd,rshd->rhts/dot_general | solution.py:76
  216.0 23.7 %multiply_reduce_fusion.2 = (f32[2,512]{1,0:T(2,128)S(1)}, f32[2,512,8,128]{1,3,2,0:T(8,128)}) fusion(f32[2,512,8]{1,2,0:T(8,128)S(1)} %get-tuple-element.166, f32[2,8,128,512]{3,2,1,0:T(8,128)} %fusion.119, f32[2,512,8,128]{3,1,2,0:T(8,128)} %copy.119, f32[2,8,512,512]{3,2,1,0:T(8,128)} %fusion.118, f32[8,512,512]{2,1,0:T(8,128)} %multiply_exponential_fusion, ...), kind=kOutput, calls=%fused_computation.99 | convolution fusion | flops 6455032832 | bytes 38309888 | tf_op jit(solution)/shard_map/rhts,rshe->rthe/dot_general | solution.py:79
  239.7 7.5 copy.123
  247.3 6.6 reshape.339
  253.9 5.4 copy.159
  259.4 7.6 multiply_reduce_fusion.1
  267.0 20.9 %fusion.19 = f32[2,1024,2816]{2,1,0:T(8,128)} fusion(bf16[1,2,1024,2816]{3,2,1,0:T(8,128)(2,1)} %all-gather.9.cloned.1.call-done, f32[1024,1024]{1,0:T(8,128)} %get-tuple-element.159, f32[1024]{0:T(1024)S(1)} %get-tuple-element.149), kind=kOutput, calls=%fused_computation.29 | convolution fusion | flops 11813257216 | bytes 38801408 | tf_op jit(solution)/shard_map/nd,kdf->knf/dot_general | solution.py:219
  287.9 14.9 %fusion.41 = (bf16[1,1024,2816]{2,1,0:T(8,128)(2,1)}, bf16[1,1024,2816]{2,1,0:T(8,128)(2,1)}) fusion(f32[2,1024,2816]{2,1,0:T(8,128)} %fusion.19, bf16[1024,1024]{1,0:T(8,128)(2,1)S(1)} %bitcast.231, bf16[1,2816,1024]{2,1,0:T(8,128)(2,1)} %all-gather.11.cloned.1.call-done), kind=kOutput, calls=%fused_computation.52 | convolution fusion | flops 5922881536 | bytes 42467328 | tf_op jit(solution)/shard_map/nd,fd->nf/dot_general | solution.py:285
  302.9 20.3 %fusion.62 = (f32[1024]{0:T(1024)S(1)}, f32[1024,1024,1]{1,0,2:T(8,128)}) fusion(f32[1024,1024]{1,0:T(8,128)} %get-tuple-element.159, bf16[1,2,1024,2816]{3,2,1,0:T(8,128)(2,1)} %all-gather.9.cloned.1.call-done, bf16[1,1024,2816]{2,1,0:T(8,128)(2,1)} %get-tuple-element.140, bf16[1,1024,2816]{2,1,0:T(8,128)(2,1)} %get-tuple-element.139), kind=kOutput, calls=%fused_computation.79 | convolution fusion | flops 11819023360 | bytes 31461376 | tf_op jit(solution)/shard_map/knf,kdf->nd/dot_general | solution.py:293
  323.1 4.7 fusion.61
  327.9 7.2 multiply_reduce_fusion
  335.1 6.3 multiply_subtract_fusion
  341.4 6.6 reshape.344
  348.0 19.9 %fusion.8 = f32[2,8,128,512]{3,2,1,0:T(8,128)} fusion(f32[2,8,512,512]{3,2,1,0:T(8,128)} %fusion.118, f32[8,512,512]{2,1,0:T(8,128)} %multiply_exponential_fusion, pred[2,512,512]{2,1,0:T(8,128)(4,1)S(1)} %compare_and_fusion, f32[2,512,8,128]{1,0,3,2:T(2,128)} %reshape.344), kind=kOutput, calls=%fused_computation.12 | convolution fusion | flops 6450839552 | bytes 34078720 | tf_op jit(solution)/shard_map/rhts,rthe->rshe/dot_general | solution.py:119
  367.9 8.9 fusion.67
  376.8 16.0 %fusion.74 = f32[2,8,512,512]{3,2,1,0:T(8,128)} fusion(f32[2,512,8,128]{3,1,2,0:T(8,128)S(1)} %copy-done.5, f32[2,512,8,128]{1,0,3,2:T(2,128)S(1)} %copy-done.6), kind=kOutput, calls=%fused_computation.107 | convolution fusion | flops 6442450944 | bytes 25165824 | tf_op jit(solution)/shard_map/rthe,rshe->rhts/dot_general | solution.py:105
  392.8 5.9 fusion.98
  398.8 43.1 %while.23 = (s32[]{:T(128)}, f32[2,8,128,128]{3,2,1,0:T(8,128)S(1)}, f32[2,8,128,128]{3,2,1,0:T(8,128)S(1)}, f32[8]{0:T(128)S(1)}, pred[2]{0:T(512)(128)(4,1)S(1)}, /*index=5*/s32[]{:T(128)}, s32[]{:T(128)}) while((s32[]{:T(128)}, f32[2,8,128,128]{3,2,1,0:T(8,128)S(1)}, f32[2,8,128,128]{3,2,1,0:T(8,128)S(1)}, f32[8]{0:T(128)S(1)}, ...), condition=%wide.region_11.12_spmd.clone, body=%wide.region_10.11_spmd.clone.sunk | while | flops 1310739 | bytes 6291745 | solution.py:143
  401.1 13.0 %collective-permute-done.1 = bf16[2,8,128,128]{3,2,1,0:T(8,128)(2,1)S(1)} collective-permute-done((bf16[2,8,128,128]{3,2,1,0:T(8,128)(2,1)}, bf16[2,8,128,128]{3,2,1,0:T(8,128)(2,1)S(1)}, u32[]{:S(2)}, u32[]{:S(2)}) %collective-permute-start.1) | collective-permute-done | bytes 524320 | tf_op jit(solution)/shard_map/while/body/eval_jaxpr/ppermute | solution.py:13
  416.6 11.7 %collective-permute-done.1 = bf16[2,8,128,128]{3,2,1,0:T(8,128)(2,1)S(1)} collective-permute-done((bf16[2,8,128,128]{3,2,1,0:T(8,128)(2,1)}, bf16[2,8,128,128]{3,2,1,0:T(8,128)(2,1)S(1)}, u32[]{:S(2)}, u32[]{:S(2)}) %collective-permute-start.1) | collective-permute-done | bytes 524320 | tf_op jit(solution)/shard_map/while/body/eval_jaxpr/ppermute | solution.py:13
  430.7 10.8 %collective-permute-done.1 = bf16[2,8,128,128]{3,2,1,0:T(8,128)(2,1)S(1)} collective-permute-done((bf16[2,8,128,128]{3,2,1,0:T(8,128)(2,1)}, bf16[2,8,128,128]{3,2,1,0:T(8,128)(2,1)S(1)}, u32[]{:S(2)}, u32[]{:S(2)}) %collective-permute-start.1) | collective-permute-done | bytes 524320 | tf_op jit(solution)/shard_map/while/body/eval_jaxpr/ppermute | solution.py:13
  441.9 8.1 fusion.123
  450.0 4.9 fusion.56
  459.8 28.1 %fusion.11 = f32[2,8,128,512]{3,2,1,0:T(8,128)} fusion(f32[2,8,512,512]{3,2,1,0:T(8,128)} %fusion.74, f32[8,512,512]{2,1,0:T(8,128)} %multiply_exponential_fusion, pred[2,512,512]{2,1,0:T(8,128)(4,1)S(1)} %compare_and_fusion, f32[2,512,8,128]{1,0,3,2:T(2,128)} %squeeze.13), kind=kOutput, calls=%fused_computation.15 | convolution fusion | flops 6455033856 | bytes 34078720 | tf_op jit(solution)/shard_map/rhts,rshd->rthd/dot_general | solution.py:107
  487.8 8.5 fusion.58
  496.3 5.3 copy.128
  501.6 6.6 reshape.345
  508.2 21.7 %fusion.57 = f32[2,512,8,128]{1,3,2,0:T(8,128)} fusion(f32[2,8,128,512]{3,2,1,0:T(8,128)} %fusion.123, f32[2,8,512,512]{3,2,1,0:T(8,128)} %fusion.74, f32[8,512,512]{2,1,0:T(8,128)} %multiply_exponential_fusion, pred[2,512,512]{2,1,0:T(8,128)(4,1)S(1)} %compare_and_fusion, f32[2,512,8]{1,2,0:T(8,128)S(1)} %copy-done.28, f32[2,512,8,128]{1,0,3,2:T(2,128)} %squeeze.12), kind=kOutput, calls=%fused_computation.70 | convolution fusion | flops 6457131008 | bytes 38305792 | tf_op jit(solution)/shard_map/rhts,rthd->rshd/dot_general | solution.py:113
  529.9 7.5 copy.131
  537.4 6.6 reshape.346
  544.1 8.3 multiply_convert_fusion.2
  554.5 11.0 %convert_bitcast_fusion.1 = bf16[4,1024,1024]{1,2,0:T(8,128)(2,1)} fusion(bf16[1024,1024]{1,0:T(8,128)(2,1)S(1)} %copy-done.22, bf16[1,1024,1024]{1,2,0:T(8,128)(2,1)S(1)} %copy-done.19, bf16[1,1024,1024]{1,2,0:T(8,128)(2,1)S(1)} %copy-done.23, bf16[1,1024,1024]{1,2,0:T(8,128)(2,1)S(1)} %get-tuple-element.142, bf16[1,1024,1024]{1,2,0:T(8,128)(2,1)S(1)} %get-tuple-element.141), kind=kOutput, calls=%fused_computation.33 | convolution fusion | flops 8606711808 | bytes 18874368 | tf_op jit(solution)/shard_map/nd,kne->kde/dot_general | solution.py:330
  565.5 15.0 %copy.151 = bf16[4,1024,1024]{2,0,1:T(4,128)(2,1)} copy(bf16[4,1024,1024]{1,2,0:T(8,128)(2,1)} %convert_bitcast_fusion.1) | data formatting | bytes 16777216
  580.5 12.3 %copy.160 = bf16[128,8,4,1024]{3,1,2,0:T(8,128)(2,1)} copy(bf16[128,8,4,1024]{3,2,1,0:T(4,128)(2,1)} %bitcast.226) | data formatting | bytes 16777216
  592.8 19.1 %convert_bitcast_fusion = bf16[2,1024,2816]{1,2,0:T(8,128)(2,1)} fusion(bf16[1,1024,2816]{2,1,0:T(8,128)(2,1)} %get-tuple-element.140, bf16[1,1024,2816]{2,1,0:T(8,128)(2,1)} %get-tuple-element.139, f32[1024,1024]{1,0:T(8,128)} %get-tuple-element.159, f32[1024]{0:T(1024)S(1)} %get-tuple-element.149), kind=kOutput, calls=%fused_computation.28 | convolution fusion | flops 11824791552 | bytes 27267072 | tf_op jit(solution)/shard_map/nd,knf->kdf/dot_general | solution.py:290
  611.9 29.1 %copy.155 = bf16[2,1024,2816]{2,0,1:T(2,128)(2,1)} copy(bf16[2,1024,2816]{1,2,0:T(8,128)(2,1)} %convert_bitcast_fusion) | data formatting | bytes 23068672
  641.0 11.4 %copy.161 = bf16[128,8,2,2816]{3,1,2,0:T(8,128)(2,1)} copy(bf16[128,8,2,2816]{3,2,1,0:T(2,128)(2,1)} %bitcast.223) | data formatting | bytes 23068672
  654.0 15.9 %fusion.45 = bf16[2816,1024]{1,0:T(8,128)(2,1)} fusion(bf16[1024,1024]{1,0:T(8,128)(2,1)S(1)} %bitcast.232, f32[2,1024,2816]{2,1,0:T(8,128)} %fusion.19), kind=kOutput, calls=%fused_computation.56 | convolution fusion | flops 5914230784 | bytes 30932992 | tf_op jit(solution)/shard_map/nf,nd->fd/dot_general | solution.py:283
  676.2 76.9 %reduce-scatter.17.cloned.1.call-done = bf16[128,5632]{1,0:T(8,128)(2,1)} async-done(((bf16[1024,5632]{1,0:T(8,128)(2,1)}), bf16[128,5632]{1,0:T(8,128)(2,1)}) %reduce-scatter.17.cloned.1.call-update) | async-done | bytes 1441808
  753.1 3.4 reshape.364
  756.5 3.1 copy.156
  759.6 56.0 %reduce-scatter.11.cloned.1.call-done = bf16[352,1024]{1,0:T(8,128)(2,1)} async-done(((bf16[2816,1024]{1,0:T(8,128)(2,1)}), bf16[352,1024]{1,0:T(8,128)(2,1)}) %reduce-scatter.11.cloned.1.call-update) | async-done | bytes 720912 | tf_op jit(solution)/shard_map/reduce_scatter | solution.py:157
  815.7 15.1 %fusion.54 = (f32[1024]{0:T(1024)S(1)}, f32[1024,1024,1]{1,0,2:T(8,128)S(1)}) fusion(bf16[2,512,1024]{2,1,0:T(8,128)(2,1)S(1)} %copy-done.12, bf16[1,5,1024,1024]{2,3,1,0:T(8,128)(2,1)} %all-gather.7.cloned.1.call-done, bf16[1,1024,1024]{1,2,0:T(8,128)(2,1)} %get-tuple-element.147, bf16[1,1024,1024]{1,2,0:T(8,128)(2,1)} %stack_reshape.4, ...), kind=kOutput, calls=%fused_computation.65 | convolution fusion | flops 8605662208 | bytes 23072768 | tf_op jit(solution)/shard_map/kne,kde->nd/dot_general | solution.py:333
  834.4 13.7 %add_convert_fusion = bf16[1024,1024]{1,0:T(8,128)(2,1)} fusion(f32[1024,1024]{1,0:T(8,128)S(1)} %copy-done.17, bf16[1,2816,1024]{2,1,0:T(8,128)(2,1)} %all-gather.11.cloned.1.call-done, f32[2,1024,2816]{2,1,0:T(8,128)} %fusion.19), kind=kOutput, calls=%fused_computation.95 | convolution fusion | flops 5913444352 | bytes 35127296 | tf_op jit(solution)/shard_map/dot_general | solution.py:17
  848.1 103.7 %all-reduce.3.cloned.1.call-done = (bf16[1,2,128,2816]{2,3,1,0:T(8,128)(2,1)}, bf16[1,128,1024]{1,2,0:T(8,128)(2,1)}, bf16[4,128,1024]{1,2,0:T(8,128)(2,1)}, bf16[1,352,1024]{2,1,0:T(8,128)(2,1)}) async-done(((bf16[1,2,128,2816]{2,3,1,0:T(8,128)(2,1)}, bf16[1,128,1024]{1,2,0:T(8,128)(2,1)}, bf16[4,128,1024]{1,2,0:T(8,128)(2,1)}, bf16[1,352,1024]{2,1,0:T(8,128)(2,1)}), (bf16[1,2,128,2816]{2,3,1,0:T(8,128)(2,1)}, ...) | async-done | bytes 3473424 | tf_op jit(solution)/shard_map/psum | solution.py:164
  955.4 3.0 copy.141
  (153 shorter events, 44.4 us)
Async XLA Ops:
  7.2 71.3 %all-gather.7.cloned.1.call-start = ((), (), s32[]{:S(2)}) async-start(), calls=%async_computation.5 | async-start | bytes 11796480 | tf_op jit(solution)/shard_map/all_gather | solution.py:193
  10.0 7.0 copy-start.10
  10.0 256.9 %all-gather.9.cloned.1.call-start = ((), (), s32[]{:S(2)}) async-start(), calls=%async_computation.6 | async-start | bytes 12976128 | tf_op jit(solution)/shard_map/all_gather | solution.py:194
  13.3 274.6 %all-gather.11.cloned.1.call-start = ((), (), s32[]{:S(2)}) async-start(), calls=%async_computation.7 | async-start | bytes 6488064 | tf_op jit(solution)/shard_map/all_gather | solution.py:195
  15.7 3.6 copy-start.36
  15.7 3.6 copy-start.35
  15.7 654.9 %reduce-scatter.15.cloned.1.call-start = ((), (), s32[]{:S(2)}) async-start(), calls=%async_computation.9 | async-start | bytes 2359296
  17.5 1.7 copy-start.29
  26.6 105.7 %copy-start.27 = (f32[2,512,8]{1,2,0:T(8,128)}, f32[2,512,8]{1,2,0:T(8,128)S(1)}, u32[]{:S(2)}) copy-start(f32[2,512,8]{1,2,0:T(8,128)S(1)} %get-tuple-element.167) | copy-start | bytes 98308
  141.9 15.3 %collective-permute-start = (bf16[2,8,128,128]{3,2,1,0:T(8,128)(2,1)}, bf16[2,8,128,128]{3,2,1,0:T(8,128)(2,1)S(1)}, u32[]{:S(2)}, u32[]{:S(2)}) collective-permute-start(bf16[2,8,128,128]{3,2,1,0:T(8,128)(2,1)} %fusion.136), channel_id=1, source_target_pairs={{0,8},{8,16},{16,24},{1,9},{9,17},{17,25},{2,10},{10,18},{18,26},{... | collective-permute-start | bytes 1572872 | tf_op jit(solution)/shard_map/while/body/eval_jaxpr/ppermute | solution.py:13
  158.4 15.4 %collective-permute-start = (bf16[2,8,128,128]{3,2,1,0:T(8,128)(2,1)}, bf16[2,8,128,128]{3,2,1,0:T(8,128)(2,1)S(1)}, u32[]{:S(2)}, u32[]{:S(2)}) collective-permute-start(bf16[2,8,128,128]{3,2,1,0:T(8,128)(2,1)} %fusion.136), channel_id=1, source_target_pairs={{0,8},{8,16},{16,24},{1,9},{9,17},{17,25},{2,10},{10,18},{18,26},{... | collective-permute-start | bytes 1572872 | tf_op jit(solution)/shard_map/while/body/eval_jaxpr/ppermute | solution.py:13
  174.9 14.5 %collective-permute-start = (bf16[2,8,128,128]{3,2,1,0:T(8,128)(2,1)}, bf16[2,8,128,128]{3,2,1,0:T(8,128)(2,1)S(1)}, u32[]{:S(2)}, u32[]{:S(2)}) collective-permute-start(bf16[2,8,128,128]{3,2,1,0:T(8,128)(2,1)} %fusion.136), channel_id=1, source_target_pairs={{0,8},{8,16},{16,24},{1,9},{9,17},{17,25},{2,10},{10,18},{18,26},{... | collective-permute-start | bytes 1572872 | tf_op jit(solution)/shard_map/while/body/eval_jaxpr/ppermute | solution.py:13
  189.5 9.2 copy-start.8
  189.5 9.2 copy-start.31
  189.5 9.2 copy-start.33
  189.5 9.2 copy-start.13
  189.5 9.2 copy-start.14
  253.9 5.5 copy-start.11
  253.9 5.5 copy-start.16
  267.0 20.9 %copy-start.24 = (bf16[2,512,1024]{2,1,0:T(8,128)(2,1)S(1)}, bf16[2,512,1024]{2,1,0:T(8,128)(2,1)}, u32[]{:S(2)}) copy-start(bf16[2,512,1024]{2,1,0:T(8,128)(2,1)} %param.17) | copy-start | bytes 6291460
  323.1 4.7 copy-start
  327.8 7.2 copy-start.2
  367.9 8.9 copy-start.5
  367.9 8.9 copy-start.6
  376.8 16.0 %copy-start.1 = (f32[128,8,2,512]{3,1,2,0:T(8,128)S(1)}, f32[128,8,2,512]{3,1,2,0:T(8,128)}, u32[]{:S(2)}) copy-start(f32[128,8,2,512]{3,1,2,0:T(8,128)} %copy.159) | copy-start | bytes 12582916
  376.8 16.0 %copy-start.3 = (f32[1024,1024]{1,0:T(8,128)S(1)}, f32[1024,1024]{1,0:T(8,128)}, u32[]{:S(2)}) copy-start(f32[1024,1024]{1,0:T(8,128)} %copy-done.2) | copy-start | bytes 12582916
  392.8 5.9 copy-start.7
  392.8 5.9 copy-start.32
  392.8 5.9 copy-start.34
  399.8 14.3 %collective-permute-start.1 = (bf16[2,8,128,128]{3,2,1,0:T(8,128)(2,1)}, bf16[2,8,128,128]{3,2,1,0:T(8,128)(2,1)S(1)}, u32[]{:S(2)}, u32[]{:S(2)}) collective-permute-start(bf16[2,8,128,128]{3,2,1,0:T(8,128)(2,1)} %fusion.137), channel_id=1, source_target_pairs={{8,0},{16,8},{24,16},{9,1},{17,9},{25,17},{10,2},{18,10},{26,18},{... | collective-permute-start | bytes 1572872 | tf_op jit(solution)/shard_map/while/body/eval_jaxpr/ppermute | solution.py:13
  415.3 13.0 %collective-permute-start.1 = (bf16[2,8,128,128]{3,2,1,0:T(8,128)(2,1)}, bf16[2,8,128,128]{3,2,1,0:T(8,128)(2,1)S(1)}, u32[]{:S(2)}, u32[]{:S(2)}) collective-permute-start(bf16[2,8,128,128]{3,2,1,0:T(8,128)(2,1)} %fusion.137), channel_id=1, source_target_pairs={{8,0},{16,8},{24,16},{9,1},{17,9},{25,17},{10,2},{18,10},{26,18},{... | collective-permute-start | bytes 1572872 | tf_op jit(solution)/shard_map/while/body/eval_jaxpr/ppermute | solution.py:13
  429.5 12.1 %collective-permute-start.1 = (bf16[2,8,128,128]{3,2,1,0:T(8,128)(2,1)}, bf16[2,8,128,128]{3,2,1,0:T(8,128)(2,1)S(1)}, u32[]{:S(2)}, u32[]{:S(2)}) collective-permute-start(bf16[2,8,128,128]{3,2,1,0:T(8,128)(2,1)} %fusion.137), channel_id=1, source_target_pairs={{8,0},{16,8},{24,16},{9,1},{17,9},{25,17},{10,2},{18,10},{26,18},{... | collective-permute-start | bytes 1572872 | tf_op jit(solution)/shard_map/while/body/eval_jaxpr/ppermute | solution.py:13
  441.9 8.1 copy-start.15
  441.9 8.1 copy-start.18
  441.9 8.1 copy-start.28
  459.8 28.1 %copy-start.9 = (f32[2,8,128,128]{3,2,1,0:T(8,128)S(1)}, f32[2,8,128,128]{3,2,1,0:T(8,128)}, u32[]{:S(2)}) copy-start(f32[2,8,128,128]{3,2,1,0:T(8,128)} %copy-done.8) | copy-start | bytes 3145732
  544.0 10.4 %copy-start.19 = (bf16[1,1024,1024]{1,2,0:T(8,128)(2,1)S(1)}, bf16[1,1024,1024]{1,2,0:T(8,128)(2,1)}, u32[]{:S(2)}) copy-start(bf16[1,1024,1024]{1,2,0:T(8,128)(2,1)} %get-tuple-element.147) | copy-start | bytes 6291460
  544.0 128.4 %reduce-scatter.13.cloned.1.call-start = ((), (), s32[]{:S(2)}) async-start(), calls=%async_computation.8 | async-start | bytes 9437184
  544.1 10.4 %copy-start.22 = (bf16[1024,1024]{1,0:T(8,128)(2,1)S(1)}, bf16[1024,1024]{1,0:T(8,128)(2,1)}, u32[]{:S(2)}) copy-start(bf16[1024,1024]{1,0:T(8,128)(2,1)} %fusion.65) | copy-start | bytes 6291460
  544.1 10.4 %copy-start.23 = (bf16[1,1024,1024]{1,2,0:T(8,128)(2,1)S(1)}, bf16[1,1024,1024]{1,2,0:T(8,128)(2,1)}, u32[]{:S(2)}) copy-start(bf16[1,1024,1024]{1,2,0:T(8,128)(2,1)} %stack_reshape.4) | copy-start | bytes 6291460
  552.4 1.4 copy-start.20
  552.4 2.0 copy-start.21
  592.7 160.4 %reduce-scatter.17.cloned.1.call-start = ((), (), s32[]{:S(2)}) async-start(), calls=%async_computation.10 | async-start | bytes 12976128
  652.4 1.6 copy-start.25
  652.4 163.2 %reduce-scatter.11.cloned.1.call-start = ((), (), s32[]{:S(2)}) async-start(), calls=%async_computation.4 | async-start | bytes 6488064 | tf_op jit(solution)/shard_map/reduce_scatter | solution.py:157
  669.9 0.7 copy-start.30
  670.0 281.8 %all-reduce.3.cloned.1.call-start = ((), (), s32[]{:S(2)}) async-start(), calls=%async_computation.11 | async-start | bytes 6946816 | tf_op jit(solution)/shard_map/psum | solution.py:164
  676.2 139.5 %copy-start.12 = (bf16[2,512,1024]{2,1,0:T(8,128)(2,1)S(1)}, bf16[2,512,1024]{2,1,0:T(8,128)(2,1)}, u32[]{:S(2)}) copy-start(bf16[2,512,1024]{2,1,0:T(8,128)(2,1)} %param.11) | copy-start | bytes 6291460
  815.7 15.1 %copy-start.4 = (f32[1024,1024]{1,0:T(8,128)S(1)}, f32[1024,1024]{1,0:T(8,128)}, u32[]{:S(2)}) copy-start(f32[1024,1024]{1,0:T(8,128)} %copy-done.2) | copy-start | bytes 12582916
  830.9 3.5 copy-start.17
  953.3 5.1 copy-start.26
Sparse Core Ops, SparseCore 0:
  10.4 67.9 all-gather.6
  80.9 67.6 all-gather.8
  150.5 43.3 all-gather.10
  544.1 40.0 reduce-scatter.14
  592.9 70.0 reduce-scatter.12
  666.3 86.8 reduce-scatter.16
  756.6 59.0 reduce-scatter.10
  819.1 132.6 all-reduce.2
where the time goes:
time: 978 us; the launch traced here: 967 us
  waiting for transfers between devices  357 us (37%)
  matrix products  343 us (35%)
  local copies, waits for them, and re-layouts  187 us (19%)
  other arithmetic  47.8 us (5%)
  starting transfers between devices  16.2 us (2%)
  between operations  15.2 us (2%)
    psum x1, waiting for transfers between devices, reduce_grads(): lax.psum(pieces[2].astype(jnp.bfloat16), 'seq').astype(jnp.float32)  104 us
    unnamed x89, local copies, waits for them, and re-layouts  98 us
    unnamed x11, waiting for transfers between devices  77.1 us
    ppermute x6, waiting for transfers between devices, passed_along(): lax.ppermute(value, axis, [(source, source + steps) for source in range(l...  68.6 us
    reduce_scatter x1, waiting for transfers between devices, reduce_grads(): lax.psum_scatter(terms[3].astype(jnp.bfloat16), 'dp', scatter_dimension=0...  56 us
    all_gather x1, waiting for transfers between devices, local(): mixer_full = lax.all_gather(gathered[0], 'dp', axis=1, tiled=True)  51.9 us
    dot_general x1, matrix products, block_back(): jnp.einsum('rhts,rshd->rthd', score_grad, per_head_keys, precision=FULL_P...  28.1 us
    dot_general x1, matrix products, block_out(): jnp.einsum('rhts,rshe->rthe', scores, per_head_values, precision=FULL_PRE...  23.7 us
  transfers between devices with their start and end apart: 14, of which 10 were waited for; matrix products, arithmetic and copies ran while one was open for 36% of the time, Pallas kernels for 0%

commit v1 on v0

--- a/solution.py
+++ b/solution.py
@@ -1,3 +1,4 @@
+import functools
 import jax
 import jax.numpy as jnp
 from jax import lax
@@ -5,6 +6,23 @@
 
 EPS = 1e-06
 FULL_PRECISION = lax.Precision.HIGHEST
+
+
+def _attach_domain(payload, which_axis):
+    num = lax.axis_size(which_axis)
+    current_value = sorted(((ii, (ii + 1) % num) for ii in range(num)))
+    t1 = payload
+    block_list = [t1]
+    for ix in range(1, num):
+        t1 = lax.ppermute(t1, which_axis, perm=current_value)
+        block_list.insert(0, t1)
+    g_now = jnp.concatenate(block_list, 1)
+    k_now = lax.axis_index(which_axis) + 1
+    local_now = jnp.roll(g_now, k_now * payload.shape[1], 1)
+    return local_now
+
+
+recast_region_in = functools.partial(_attach_domain, which_axis="dp")
 
 
 def passed_along(value, axis, steps):
@@ -190,7 +208,7 @@
         channel_in_weights[layer_index].astype(jnp.bfloat16),
         channel_out_weights[layer_index].astype(jnp.bfloat16),
     )
-    mixer_full = lax.all_gather(gathered[0], "dp", axis=1, tiled=True)
+    mixer_full = recast_region_in(gathered[0])
     channel_full = lax.all_gather(gathered[1], "dp", axis=1, tiled=True)
     down_full = lax.all_gather(gathered[2], "dp", axis=0, tiled=True)
     normed, factor_in = rms_norm(resid)

time: 978 us -> 1140 us (1.17)
  waiting for transfers between devices: 357 us -> 464 us
  local copies, waits for them, and re-layouts: 187 us -> 221 us
  starting transfers between devices: 16.2 us -> 32.9 us
    ppermute x0 -> x7, waiting for transfers between devices: none -> 165 us  [_attach_domain(): t1 = lax.ppermute(t1, which_axis, perm=current_value)]
    all_gather x1 -> x0, waiting for transfers between devices: 51.9 us -> none  [local(): mixer_full = lax.all_gather(gathered[0], 'dp', axis=1, tiled=True)]
    unnamed x89 -> x122, local copies, waits for them, and re-layouts: 98 us -> 131 us
    unnamed x11 -> x10, waiting for transfers between devices: 77.1 us -> 77.2 us
  transfers between devices with their start and end apart: 14 -> 20, of which waited for: 10 -> 16; matrix products, arithmetic and copies ran while one was open for 36% -> 34% of each run, Pallas kernels for 0% -> 0%
where the time goes in v1:
time: 1140 us; the launch traced here: 1130 us
  waiting for transfers between devices  464 us (41%)
  matrix products  342 us (30%)
  local copies, waits for them, and re-layouts  221 us (19%)
  other arithmetic  51.8 us (5%)
  starting transfers between devices  32.9 us (3%)
  between operations  15.2 us (1%)
    ppermute x7, waiting for transfers between devices, _attach_domain(): t1 = lax.ppermute(t1, which_axis, perm=current_value)  165 us
    unnamed x122, local copies, waits for them, and re-layouts  131 us
    psum x1, waiting for transfers between devices, reduce_grads(): lax.psum(pieces[2].astype(jnp.bfloat16), 'seq').astype(jnp.float32)  105 us
    unnamed x10, waiting for transfers between devices  77.2 us
    ppermute x6, waiting for transfers between devices, passed_along(): lax.ppermute(value, axis, [(source, source + steps) for source in range(l...  61.3 us
    reduce_scatter x1, waiting for transfers between devices, reduce_grads(): lax.psum_scatter(terms[3].astype(jnp.bfloat16), 'dp', scatter_dimension=0...  55.9 us
    dot_general x1, matrix products, block_back(): jnp.einsum('rhts,rshd->rthd', score_grad, per_head_keys, precision=FULL_P...  27.9 us
    ppermute x6, starting transfers between devices, passed_along(): lax.ppermute(value, axis, [(source, source + steps) for source in range(l...  27.2 us
  transfers between devices with their start and end apart: 20, of which 16 were waited for; matrix products, arithmetic and copies ran while one was open for 34% of the time, Pallas kernels for 0%

profile of v1, /device:TPU:0, one launch (start us, length us, event | category | flops | bytes accessed | tf_op | source)
XLA Modules:
  0.0 1128.2 jit_solution(1122919101500040450)
XLA Ops:
  13.8 32.4 %collective-permute-done.2 = bf16[5,128,1024]{1,2,0:T(8,128)(2,1)S(1)} collective-permute-done((bf16[5,128,1024]{1,2,0:T(8,128)(2,1)}, bf16[5,128,1024]{1,2,0:T(8,128)(2,1)S(1)}, u32[]{:S(2)}, u32[]{:S(2)}) %collective-permute-start.2) | collective-permute-done | bytes 1310752 | tf_op jit(solution)/shard_map/ppermute | solution.py:17
  47.7 35.5 %collective-permute-done.3 = bf16[5,128,1024]{1,2,0:T(8,128)(2,1)S(1)} collective-permute-done((bf16[5,128,1024]{1,2,0:T(8,128)(2,1)S(1)}, bf16[5,128,1024]{1,2,0:T(8,128)(2,1)S(1)}, u32[]{:S(2)}, u32[]{:S(2)}) %collective-permute-start.3) | collective-permute-done | bytes 1310752 | tf_op jit(solution)/shard_map/ppermute | solution.py:17
  88.8 21.3 %collective-permute-done.4 = bf16[5,128,1024]{1,2,0:T(8,128)(2,1)S(1)} collective-permute-done((bf16[5,128,1024]{1,2,0:T(8,128)(2,1)S(1)}, bf16[5,128,1024]{1,2,0:T(8,128)(2,1)S(1)}, u32[]{:S(2)}, u32[]{:S(2)}) %collective-permute-start.4) | collective-permute-done | bytes 1310752 | tf_op jit(solution)/shard_map/ppermute | solution.py:17
  111.1 18.0 %collective-permute-done.5 = bf16[5,128,1024]{1,2,0:T(8,128)(2,1)} collective-permute-done((bf16[5,128,1024]{1,2,0:T(8,128)(2,1)S(1)}, bf16[5,128,1024]{1,2,0:T(8,128)(2,1)}, u32[]{:S(2)}, u32[]{:S(2)}) %collective-permute-start.5) | collective-permute-done | bytes 1310752 | tf_op jit(solution)/shard_map/ppermute | solution.py:17
  132.3 16.4 %collective-permute-done.6 = bf16[5,128,1024]{1,2,0:T(8,128)(2,1)} collective-permute-done((bf16[5,128,1024]{1,2,0:T(8,128)(2,1)}, bf16[5,128,1024]{1,2,0:T(8,128)(2,1)}, u32[]{:S(2)}, u32[]{:S(2)}) %collective-permute-start.6) | collective-permute-done | bytes 1310752 | tf_op jit(solution)/shard_map/ppermute | solution.py:17
  150.5 24.8 %collective-permute-done.7 = bf16[5,128,1024]{1,2,0:T(8,128)(2,1)} collective-permute-done((bf16[5,128,1024]{1,2,0:T(8,128)(2,1)}, bf16[5,128,1024]{1,2,0:T(8,128)(2,1)}, u32[]{:S(2)}, u32[]{:S(2)}) %collective-permute-start.7) | collective-permute-done | bytes 1310752 | tf_op jit(solution)/shard_map/ppermute | solution.py:17
  181.8 16.9 %collective-permute-done.8 = bf16[5,128,1024]{1,2,0:T(8,128)(2,1)} collective-permute-done((bf16[5,128,1024]{1,2,0:T(8,128)(2,1)}, bf16[5,128,1024]{1,2,0:T(8,128)(2,1)}, u32[]{:S(2)}, u32[]{:S(2)}) %collective-permute-start.8) | collective-permute-done | bytes 1310752 | tf_op jit(solution)/shard_map/ppermute | solution.py:17
  229.5 14.9 %fusion.24 = f32[4,1024,1024]{1,2,0:T(8,128)} fusion(bf16[5,2048,1024]{1,2,0:T(8,128)(2,1)} %constant_dynamic-update-slice_fusion, s32[]{:T(128)S(6)} %select_n.37, bf16[1024,1024]{1,0:T(8,128)(2,1)S(1)} %fusion.71), kind=kOutput, calls=%fused_computation.32 | convolution fusion | flops 8589934592 | bytes 29360132 | tf_op jit(solution)/shard_map/nd,kde->kne/dot_general | solution.py:216
  244.3 10.1 fusion.130
  254.4 6.6 reshape_squeeze.3
  261.0 7.2 copy.119
  268.2 6.6 squeeze.13
  274.8 7.0 squeeze.12
  281.8 9.6 fusion.75
  291.3 60.7 %while.22 = (s32[]{:T(128)}, f32[2,8,128,128]{3,2,1,0:T(8,128)S(1)}, f32[2,8,128,128]{3,2,1,0:T(8,128)}, f32[8]{0:T(128)S(1)}, pred[2]{0:T(512)(128)(4,1)S(1)}, /*index=5*/s32[]{:T(128)}, s32[]{:T(128)}) while((s32[]{:T(128)}, f32[2,8,128,128]{3,2,1,0:T(8,128)S(1)}, f32[2,8,128,128]{3,2,1,0:T(8,128)}, f32[8]{0:T(128)S(1)}, ...), condition=%wide.region_5.6_spmd.clone, body=%wide.region_4.5_spmd.clone.sunk | while | flops 1310739 | bytes 6291745 | solution.py:152
  293.6 12.8 %collective-permute-start = (bf16[2,8,128,128]{3,2,1,0:T(8,128)(2,1)}, bf16[2,8,128,128]{3,2,1,0:T(8,128)(2,1)}, u32[]{:S(2)}, u32[]{:S(2)}) collective-permute-start(bf16[2,8,128,128]{3,2,1,0:T(8,128)(2,1)} %fusion.146), channel_id=1, source_target_pairs={{0,8},{8,16},{16,24},{1,9},{9,17},{17,25},{2,10},{10,18},{18,26},{... | collective-permute-start | bytes 1572872 | tf_op jit(solution)/shard_map/while/body/eval_jaxpr/ppermute | solution.py:31
  306.4 9.8 collective-permute-done
  319.7 5.2 collective-permute-start
  324.9 11.0 collective-permute-done
  339.3 5.4 collective-permute-start
  344.7 6.2 collective-permute-done
  352.1 9.1 fusion.129
  361.2 17.0 %fusion.128 = f32[2,8,512,512]{3,2,1,0:T(8,128)} fusion(f32[2,512,8,128]{1,0,3,2:T(2,128)S(1)} %copy-done.15, f32[2,512,8,128]{1,0,3,2:T(2,128)S(1)} %copy-done.14), kind=kOutput, calls=%fused_computation.187 | convolution fusion | flops 6450839552 | bytes 25165824 | tf_op jit(solution)/shard_map/rthd,rshd->rhts/dot_general | solution.py:94
  378.3 23.8 %multiply_reduce_fusion.2 = (f32[2,512]{1,0:T(2,128)S(1)}, f32[2,512,8,128]{1,3,2,0:T(8,128)}) fusion(f32[2,512,8]{1,2,0:T(8,128)S(1)} %get-tuple-element.166, f32[2,8,128,512]{3,2,1,0:T(8,128)} %fusion.129, f32[2,512,8,128]{3,1,2,0:T(8,128)} %copy.119, f32[2,8,512,512]{3,2,1,0:T(8,128)} %fusion.128, f32[8,512,512]{2,1,0:T(8,128)} %multiply_exponential_fusion, ...), kind=kOutput, calls=%fused_computation.101 | convolution fusion | flops 6455032832 | bytes 38309888 | tf_op jit(solution)/shard_map/rhts,rshe->rthe/dot_general | solution.py:97
  402.1 7.4 copy.123
  409.4 6.6 reshape.339
  416.1 5.4 copy.159
  421.5 7.6 multiply_reduce_fusion.1
  429.1 21.3 %fusion.21 = f32[2,1024,2816]{2,1,0:T(8,128)} fusion(bf16[1,2,1024,2816]{3,2,1,0:T(8,128)(2,1)} %all-gather.5.cloned.1.call-done, f32[1024,1024]{1,0:T(8,128)} %get-tuple-element.159, f32[1024]{0:T(1024)S(1)} %get-tuple-element.149), kind=kOutput, calls=%fused_computation.31 | convolution fusion | flops 11813257216 | bytes 38801408 | tf_op jit(solution)/shard_map/nd,kdf->knf/dot_general | solution.py:237
  450.4 15.0 %fusion.47 = (bf16[1,1024,2816]{2,1,0:T(8,128)(2,1)}, bf16[1,1024,2816]{2,1,0:T(8,128)(2,1)}) fusion(f32[2,1024,2816]{2,1,0:T(8,128)} %fusion.21, bf16[1024,1024]{1,0:T(8,128)(2,1)S(1)} %bitcast.231, bf16[1,2816,1024]{2,1,0:T(8,128)(2,1)} %all-gather.7.cloned.1.call-done), kind=kOutput, calls=%fused_computation.54 | convolution fusion | flops 5922881536 | bytes 42467328 | tf_op jit(solution)/shard_map/nd,fd->nf/dot_general | solution.py:303
  465.5 20.3 %fusion.68 = (f32[1024]{0:T(1024)S(1)}, f32[1024,1024,1]{1,0,2:T(8,128)}) fusion(f32[1024,1024]{1,0:T(8,128)} %get-tuple-element.159, bf16[1,2,1024,2816]{3,2,1,0:T(8,128)(2,1)} %all-gather.5.cloned.1.call-done, bf16[1,1024,2816]{2,1,0:T(8,128)(2,1)} %get-tuple-element.140, bf16[1,1024,2816]{2,1,0:T(8,128)(2,1)} %get-tuple-element.139), kind=kOutput, calls=%fused_computation.81 | convolution fusion | flops 11819023360 | bytes 31461376 | tf_op jit(solution)/shard_map/knf,kdf->nd/dot_general | solution.py:311
  490.4 7.1 multiply_reduce_fusion
  497.5 6.3 multiply_subtract_fusion
  503.7 6.7 reshape.344
  510.4 19.9 %fusion.8 = f32[2,8,128,512]{3,2,1,0:T(8,128)} fusion(f32[2,8,512,512]{3,2,1,0:T(8,128)} %fusion.128, f32[8,512,512]{2,1,0:T(8,128)} %multiply_exponential_fusion, pred[2,512,512]{2,1,0:T(8,128)(4,1)S(1)} %copy-done.17, f32[2,512,8,128]{1,0,3,2:T(2,128)} %reshape.344), kind=kOutput, calls=%fused_computation.12 | convolution fusion | flops 6450839552 | bytes 34078720 | tf_op jit(solution)/shard_map/rhts,rthe->rshe/dot_general | solution.py:137
  530.3 8.8 fusion.73
  539.2 16.0 %fusion.80 = f32[2,8,512,512]{3,2,1,0:T(8,128)} fusion(f32[2,512,8,128]{3,1,2,0:T(8,128)S(1)} %copy-done.5, f32[2,512,8,128]{1,0,3,2:T(2,128)S(1)} %copy-done.6), kind=kOutput, calls=%fused_computation.109 | convolution fusion | flops 6442450944 | bytes 25165824 | tf_op jit(solution)/shard_map/rthe,rshe->rhts/dot_general | solution.py:123
  555.2 5.9 fusion.104
  561.1 42.1 %while.23 = (s32[]{:T(128)}, f32[2,8,128,128]{3,2,1,0:T(8,128)S(1)}, f32[2,8,128,128]{3,2,1,0:T(8,128)S(1)}, f32[8]{0:T(128)S(1)}, pred[2]{0:T(512)(128)(4,1)S(1)}, /*index=5*/s32[]{:T(128)}, s32[]{:T(128)}) while((s32[]{:T(128)}, f32[2,8,128,128]{3,2,1,0:T(8,128)S(1)}, f32[2,8,128,128]{3,2,1,0:T(8,128)S(1)}, f32[8]{0:T(128)S(1)}, ...), condition=%wide.region_11.12_spmd.clone, body=%wide.region_10.11_spmd.clone.sunk | while | flops 1310739 | bytes 6291745 | solution.py:161
  563.5 12.9 %collective-permute-done.1 = bf16[2,8,128,128]{3,2,1,0:T(8,128)(2,1)S(1)} collective-permute-done((bf16[2,8,128,128]{3,2,1,0:T(8,128)(2,1)}, bf16[2,8,128,128]{3,2,1,0:T(8,128)(2,1)S(1)}, u32[]{:S(2)}, u32[]{:S(2)}) %collective-permute-start.1) | collective-permute-done | bytes 524320 | tf_op jit(solution)/shard_map/while/body/eval_jaxpr/ppermute | solution.py:31
  578.8 11.5 %collective-permute-done.1 = bf16[2,8,128,128]{3,2,1,0:T(8,128)(2,1)S(1)} collective-permute-done((bf16[2,8,128,128]{3,2,1,0:T(8,128)(2,1)}, bf16[2,8,128,128]{3,2,1,0:T(8,128)(2,1)S(1)}, u32[]{:S(2)}, u32[]{:S(2)}) %collective-permute-start.1) | collective-permute-done | bytes 524320 | tf_op jit(solution)/shard_map/while/body/eval_jaxpr/ppermute | solution.py:31
  592.8 10.0 collective-permute-done.1
  603.3 8.1 fusion.133
  611.4 4.9 fusion.62
  621.1 27.9 %fusion.11 = f32[2,8,128,512]{3,2,1,0:T(8,128)} fusion(f32[2,8,512,512]{3,2,1,0:T(8,128)} %fusion.80, f32[8,512,512]{2,1,0:T(8,128)} %multiply_exponential_fusion, pred[2,512,512]{2,1,0:T(8,128)(4,1)S(1)} %copy-done.17, f32[2,512,8,128]{1,0,3,2:T(2,128)} %squeeze.13), kind=kOutput, calls=%fused_computation.15 | convolution fusion | flops 6455033856 | bytes 34078720 | tf_op jit(solution)/shard_map/rhts,rshd->rthd/dot_general | solution.py:125
  649.1 8.5 fusion.64
  657.6 5.2 copy.128
  662.8 6.6 reshape.345
  669.4 21.8 %fusion.63 = f32[2,512,8,128]{1,3,2,0:T(8,128)} fusion(f32[2,8,128,512]{3,2,1,0:T(8,128)} %fusion.133, f32[2,8,512,512]{3,2,1,0:T(8,128)} %fusion.80, f32[8,512,512]{2,1,0:T(8,128)} %multiply_exponential_fusion, pred[2,512,512]{2,1,0:T(8,128)(4,1)S(1)} %copy-done.17, f32[2,512,8]{1,2,0:T(8,128)S(1)} %copy-done.37, f32[2,512,8,128]{1,0,3,2:T(2,128)} %squeeze.12), kind=kOutput, calls=%fused_computation.72 | convolution fusion | flops 6457131008 | bytes 38305792 | tf_op jit(solution)/shard_map/rhts,rthd->rshd/dot_general | solution.py:131
  691.2 7.5 copy.131
  698.6 6.6 reshape.346
  705.4 7.8 multiply_convert_fusion.2
  715.2 11.1 convert_bitcast_fusion.1
  726.3 14.9 %copy.151 = bf16[4,1024,1024]{2,0,1:T(4,128)(2,1)} copy(bf16[4,1024,1024]{1,2,0:T(8,128)(2,1)} %convert_bitcast_fusion.1) | data formatting | bytes 16777216
  741.2 12.1 %copy.160 = bf16[128,8,4,1024]{3,1,2,0:T(8,128)(2,1)} copy(bf16[128,8,4,1024]{3,2,1,0:T(4,128)(2,1)} %bitcast.225) | data formatting | bytes 16777216
  753.4 19.5 %convert_bitcast_fusion = bf16[2,1024,2816]{1,2,0:T(8,128)(2,1)} fusion(bf16[1,1024,2816]{2,1,0:T(8,128)(2,1)} %get-tuple-element.140, bf16[1,1024,2816]{2,1,0:T(8,128)(2,1)} %get-tuple-element.139, f32[1024,1024]{1,0:T(8,128)} %get-tuple-element.159, f32[1024]{0:T(1024)S(1)} %get-tuple-element.149), kind=kOutput, calls=%fused_computation.28 | convolution fusion | flops 11824791552 | bytes 27267072 | tf_op jit(solution)/shard_map/nd,knf->kdf/dot_general | solution.py:308
  772.9 29.3 %copy.155 = bf16[2,1024,2816]{2,0,1:T(2,128)(2,1)} copy(bf16[2,1024,2816]{1,2,0:T(8,128)(2,1)} %convert_bitcast_fusion) | data formatting | bytes 23068672
  802.2 11.4 %copy.161 = bf16[128,8,2,2816]{3,1,2,0:T(8,128)(2,1)} copy(bf16[128,8,2,2816]{3,2,1,0:T(2,128)(2,1)} %bitcast.222) | data formatting | bytes 23068672
  815.1 16.0 %fusion.51 = bf16[2816,1024]{1,0:T(8,128)(2,1)} fusion(bf16[1024,1024]{1,0:T(8,128)(2,1)S(1)} %bitcast.232, f32[2,1024,2816]{2,1,0:T(8,128)} %fusion.21), kind=kOutput, calls=%fused_computation.58 | convolution fusion | flops 5914230784 | bytes 30932992 | tf_op jit(solution)/shard_map/nf,nd->fd/dot_general | solution.py:301
  837.4 77.1 %reduce-scatter.17.cloned.1.call-done = bf16[128,5632]{1,0:T(8,128)(2,1)} async-done(((bf16[1024,5632]{1,0:T(8,128)(2,1)}), bf16[128,5632]{1,0:T(8,128)(2,1)}) %reduce-scatter.17.cloned.1.call-update) | async-done | bytes 1441808
  921.1 55.9 %reduce-scatter.11.cloned.1.call-done = bf16[352,1024]{1,0:T(8,128)(2,1)} async-done(((bf16[2816,1024]{1,0:T(8,128)(2,1)}), bf16[352,1024]{1,0:T(8,128)(2,1)}) %reduce-scatter.11.cloned.1.call-update) | async-done | bytes 720912 | tf_op jit(solution)/shard_map/reduce_scatter | solution.py:175
  977.0 14.4 %fusion.60 = (f32[1024]{0:T(1024)S(1)}, f32[1024,1024,1]{1,0,2:T(8,128)S(1)}) fusion(bf16[2,512,1024]{2,1,0:T(8,128)(2,1)S(1)} %copy-done.11, bf16[5,2048,1024]{1,2,0:T(8,128)(2,1)} %constant_dynamic-update-slice_fusion, s32[]{:T(128)S(6)} %select_n.37, bf16[1,1024,1024]{1,2,0:T(8,128)(2,1)} %get-tuple-element.147, ...), kind=kOutput, calls=%fused_computation.67 | convolution fusion | flops 8605662208 | bytes 23072772 | tf_op jit(solution)/shard_map/kne,kde->nd/dot_general | solution.py:351
  994.9 13.5 %add_convert_fusion = bf16[1024,1024]{1,0:T(8,128)(2,1)} fusion(f32[1024,1024]{1,0:T(8,128)S(1)} %copy-done.13, bf16[1,2816,1024]{2,1,0:T(8,128)(2,1)} %all-gather.7.cloned.1.call-done, f32[2,1024,2816]{2,1,0:T(8,128)} %fusion.21), kind=kOutput, calls=%fused_computation.97 | convolution fusion | flops 5913444352 | bytes 35127296 | tf_op jit(solution)/shard_map/dot_general | solution.py:35
  1008.3 104.7 %all-reduce.3.cloned.1.call-done = (bf16[1,2,128,2816]{2,3,1,0:T(8,128)(2,1)}, bf16[1,128,1024]{1,2,0:T(8,128)(2,1)}, bf16[4,128,1024]{1,2,0:T(8,128)(2,1)}, bf16[1,352,1024]{2,1,0:T(8,128)(2,1)}) async-done(((bf16[1,2,128,2816]{2,3,1,0:T(8,128)(2,1)}, bf16[1,128,1024]{1,2,0:T(8,128)(2,1)}, bf16[4,128,1024]{1,2,0:T(8,128)(2,1)}, bf16[1,352,1024]{2,1,0:T(8,128)(2,1)}), (bf16[1,2,128,2816]{2,3,1,0:T(8,128)(2,1)}, ...) | async-done | bytes 3473424 | tf_op jit(solution)/shard_map/psum | solution.py:182
  (198 shorter events, 111.7 us)
Async XLA Ops:
  7.2 421.9 %all-gather.5.cloned.1.call-start = ((), (), s32[]{:S(2)}) async-start(), calls=%async_computation.5 | async-start | bytes 12976128 | tf_op jit(solution)/shard_map/all_gather | solution.py:212
  10.3 121.3 %copy-start.44 = (s32[2,4]{1,0:T(2,128)S(1)}, s32[2,4]{1,0:T(2,128)}, u32[]{:S(2)}) copy-start(s32[2,4]{1,0:T(2,128)} %param.16) | copy-start | bytes 100
  10.3 139.6 %copy-start.45 = (f32[1,8]{1,0:T(1,128)S(1)}, f32[1,8]{1,0:T(1,128)}, u32[]{:S(2)}) copy-start(f32[1,8]{1,0:T(1,128)} %param.15) | copy-start | bytes 100
  10.3 139.6 %copy-start.10 = (bf16[2,512,1024]{2,1,0:T(8,128)(2,1)S(1)}, bf16[2,512,1024]{2,1,0:T(8,128)(2,1)}, u32[]{:S(2)}) copy-start(bf16[2,512,1024]{2,1,0:T(8,128)(2,1)} %param.11) | copy-start | bytes 6291460
  10.3 440.1 %all-gather.7.cloned.1.call-start = ((), (), s32[]{:S(2)}) async-start(), calls=%async_computation.6 | async-start | bytes 6488064 | tf_op jit(solution)/shard_map/all_gather | solution.py:213
  13.3 32.8 %collective-permute-start.2 = (bf16[5,128,1024]{1,2,0:T(8,128)(2,1)}, bf16[5,128,1024]{1,2,0:T(8,128)(2,1)S(1)}, u32[]{:S(2)}, u32[]{:S(2)}) collective-permute-start(bf16[5,128,1024]{1,2,0:T(8,128)(2,1)} %bitcast.226), channel_id=1, source_target_pairs={{0,1},{1,2},{2,3},{3,4},{4,5},{5,6},{6,7},{7,0},{8,9},{9,10},{10,1... | collective-permute-start | bytes 3932168 | tf_op jit(solution)/shard_map/ppermute | solution.py:17
  46.1 1.1 copy-start.19
  47.2 36.1 %collective-permute-start.3 = (bf16[5,128,1024]{1,2,0:T(8,128)(2,1)S(1)}, bf16[5,128,1024]{1,2,0:T(8,128)(2,1)S(1)}, u32[]{:S(2)}, u32[]{:S(2)}) collective-permute-start(bf16[5,128,1024]{1,2,0:T(8,128)(2,1)S(1)} %collective-permute-done.2), channel_id=1, source_target_pairs={{0,1},{1,2},{2,3},{3,4},{4,5},{5,6},{6,7},{7,0},{8,9},{9,10},{10,1... | collective-permute-start | bytes 3932168 | tf_op jit(solution)/shard_map/ppermute | solution.py:17
  84.3 25.7 %collective-permute-start.4 = (bf16[5,128,1024]{1,2,0:T(8,128)(2,1)S(1)}, bf16[5,128,1024]{1,2,0:T(8,128)(2,1)S(1)}, u32[]{:S(2)}, u32[]{:S(2)}) collective-permute-start(bf16[5,128,1024]{1,2,0:T(8,128)(2,1)S(1)} %collective-permute-done.3), channel_id=1, source_target_pairs={{0,1},{1,2},{2,3},{3,4},{4,5},{5,6},{6,7},{7,0},{8,9},{9,10},{10,1... | collective-permute-start | bytes 3932168 | tf_op jit(solution)/shard_map/ppermute | solution.py:17
  110.1 1.1 copy-start.23
  111.1 18.0 %collective-permute-start.5 = (bf16[5,128,1024]{1,2,0:T(8,128)(2,1)S(1)}, bf16[5,128,1024]{1,2,0:T(8,128)(2,1)}, u32[]{:S(2)}, u32[]{:S(2)}) collective-permute-start(bf16[5,128,1024]{1,2,0:T(8,128)(2,1)S(1)} %collective-permute-done.4), channel_id=1, source_target_pairs={{0,1},{1,2},{2,3},{3,4},{4,5},{5,6},{6,7},{7,0},{8,9},{9,10},{10,1... | collective-permute-start | bytes 3932168 | tf_op jit(solution)/shard_map/ppermute | solution.py:17
  129.2 19.5 %collective-permute-start.6 = (bf16[5,128,1024]{1,2,0:T(8,128)(2,1)}, bf16[5,128,1024]{1,2,0:T(8,128)(2,1)}, u32[]{:S(2)}, u32[]{:S(2)}) collective-permute-start(bf16[5,128,1024]{1,2,0:T(8,128)(2,1)} %collective-permute-done.5), channel_id=1, source_target_pairs={{0,1},{1,2},{2,3},{3,4},{4,5},{5,6},{6,7},{7,0},{8,9},{9,10},{10,1... | collective-permute-start | bytes 3932168 | tf_op jit(solution)/shard_map/ppermute | solution.py:17
  131.5 700.3 %reduce-scatter.15.cloned.1.call-start = ((), (), s32[]{:S(2)}) async-start(), calls=%async_computation.8 | async-start | bytes 2359296
  148.6 26.7 %collective-permute-start.7 = (bf16[5,128,1024]{1,2,0:T(8,128)(2,1)}, bf16[5,128,1024]{1,2,0:T(8,128)(2,1)}, u32[]{:S(2)}, u32[]{:S(2)}) collective-permute-start(bf16[5,128,1024]{1,2,0:T(8,128)(2,1)} %collective-permute-done.6), channel_id=1, source_target_pairs={{0,1},{1,2},{2,3},{3,4},{4,5},{5,6},{6,7},{7,0},{8,9},{9,10},{10,1... | collective-permute-start | bytes 3932168 | tf_op jit(solution)/shard_map/ppermute | solution.py:17
  175.3 23.4 %collective-permute-start.8 = (bf16[5,128,1024]{1,2,0:T(8,128)(2,1)}, bf16[5,128,1024]{1,2,0:T(8,128)(2,1)}, u32[]{:S(2)}, u32[]{:S(2)}) collective-permute-start(bf16[5,128,1024]{1,2,0:T(8,128)(2,1)} %collective-permute-done.7), channel_id=1, source_target_pairs={{0,1},{1,2},{2,3},{3,4},{4,5},{5,6},{6,7},{7,0},{8,9},{9,10},{10,1... | collective-permute-start | bytes 3932168 | tf_op jit(solution)/shard_map/ppermute | solution.py:17
  175.6 6.2 copy-start.38
  175.6 1.7 copy-start.25
  175.6 106.2 %copy-start.36 = (f32[2,512,8]{1,2,0:T(8,128)}, f32[2,512,8]{1,2,0:T(8,128)S(1)}, u32[]{:S(2)}) copy-start(f32[2,512,8]{1,2,0:T(8,128)S(1)} %get-tuple-element.167) | copy-start | bytes 98308
  177.3 52.2 %copy-start.30 = (bf16[1024,1024]{1,0:T(8,128)(2,1)}, bf16[1024,1024]{1,0:T(8,128)(2,1)S(1)}, u32[]{:S(2)}) copy-start(bf16[1024,1024]{1,0:T(8,128)(2,1)S(1)} %fusion.71) | copy-start | bytes 6291460
  201.2 8.0 copy-start.24
  203.9 6.7 copy-start.22
  206.6 5.2 copy-start.20
  209.2 3.8 copy-start.18
  293.6 22.6 %collective-permute-start = (bf16[2,8,128,128]{3,2,1,0:T(8,128)(2,1)}, bf16[2,8,128,128]{3,2,1,0:T(8,128)(2,1)}, u32[]{:S(2)}, u32[]{:S(2)}) collective-permute-start(bf16[2,8,128,128]{3,2,1,0:T(8,128)(2,1)} %fusion.146), channel_id=1, source_target_pairs={{0,8},{8,16},{16,24},{1,9},{9,17},{17,25},{2,10},{10,18},{18,26},{... | collective-permute-start | bytes 1572872 | tf_op jit(solution)/shard_map/while/body/eval_jaxpr/ppermute | solution.py:31
  319.7 16.2 %collective-permute-start = (bf16[2,8,128,128]{3,2,1,0:T(8,128)(2,1)}, bf16[2,8,128,128]{3,2,1,0:T(8,128)(2,1)}, u32[]{:S(2)}, u32[]{:S(2)}) collective-permute-start(bf16[2,8,128,128]{3,2,1,0:T(8,128)(2,1)} %fusion.146), channel_id=1, source_target_pairs={{0,8},{8,16},{16,24},{1,9},{9,17},{17,25},{2,10},{10,18},{18,26},{... | collective-permute-start | bytes 1572872 | tf_op jit(solution)/shard_map/while/body/eval_jaxpr/ppermute | solution.py:31
  339.3 11.6 %collective-permute-start = (bf16[2,8,128,128]{3,2,1,0:T(8,128)(2,1)}, bf16[2,8,128,128]{3,2,1,0:T(8,128)(2,1)}, u32[]{:S(2)}, u32[]{:S(2)}) collective-permute-start(bf16[2,8,128,128]{3,2,1,0:T(8,128)(2,1)} %fusion.146), channel_id=1, source_target_pairs={{0,8},{8,16},{16,24},{1,9},{9,17},{17,25},{2,10},{10,18},{18,26},{... | collective-permute-start | bytes 1572872 | tf_op jit(solution)/shard_map/while/body/eval_jaxpr/ppermute | solution.py:31
  352.0 9.2 copy-start.8
  352.0 9.2 copy-start.40
  352.0 9.2 copy-start.42
  352.1 9.2 copy-start.14
  352.1 9.2 copy-start.15
  416.1 5.4 copy-start.12
  429.1 21.3 %copy-start.33 = (bf16[2,512,1024]{2,1,0:T(8,128)(2,1)S(1)}, bf16[2,512,1024]{2,1,0:T(8,128)(2,1)}, u32[]{:S(2)}) copy-start(bf16[2,512,1024]{2,1,0:T(8,128)(2,1)} %param.17) | copy-start | bytes 6291460
  485.7 4.7 copy-start
  490.2 7.2 copy-start.2
  503.7 6.7 copy-start.17
  530.3 8.9 copy-start.5
  530.3 8.9 copy-start.6
  539.2 16.0 %copy-start.1 = (f32[128,8,2,512]{3,1,2,0:T(8,128)S(1)}, f32[128,8,2,512]{3,1,2,0:T(8,128)}, u32[]{:S(2)}) copy-start(f32[128,8,2,512]{3,1,2,0:T(8,128)} %copy.159) | copy-start | bytes 12582916
  539.2 16.0 %copy-start.3 = (f32[1024,1024]{1,0:T(8,128)S(1)}, f32[1024,1024]{1,0:T(8,128)}, u32[]{:S(2)}) copy-start(f32[1024,1024]{1,0:T(8,128)} %copy-done.2) | copy-start | bytes 12582916
  555.2 6.0 copy-start.7
  555.2 6.0 copy-start.41
  555.2 5.9 copy-start.43
  562.2 14.1 %collective-permute-start.1 = (bf16[2,8,128,128]{3,2,1,0:T(8,128)(2,1)}, bf16[2,8,128,128]{3,2,1,0:T(8,128)(2,1)S(1)}, u32[]{:S(2)}, u32[]{:S(2)}) collective-permute-start(bf16[2,8,128,128]{3,2,1,0:T(8,128)(2,1)} %fusion.147), channel_id=1, source_target_pairs={{8,0},{16,8},{24,16},{9,1},{17,9},{25,17},{10,2},{18,10},{26,18},{... | collective-permute-start | bytes 1572872 | tf_op jit(solution)/shard_map/while/body/eval_jaxpr/ppermute | solution.py:31
  577.5 12.8 %collective-permute-start.1 = (bf16[2,8,128,128]{3,2,1,0:T(8,128)(2,1)}, bf16[2,8,128,128]{3,2,1,0:T(8,128)(2,1)S(1)}, u32[]{:S(2)}, u32[]{:S(2)}) collective-permute-start(bf16[2,8,128,128]{3,2,1,0:T(8,128)(2,1)} %fusion.147), channel_id=1, source_target_pairs={{8,0},{16,8},{24,16},{9,1},{17,9},{25,17},{10,2},{18,10},{26,18},{... | collective-permute-start | bytes 1572872 | tf_op jit(solution)/shard_map/while/body/eval_jaxpr/ppermute | solution.py:31
  591.5 11.3 collective-permute-start.1
  603.3 8.1 copy-start.16
  603.3 8.1 copy-start.26
  603.3 8.1 copy-start.37
  621.1 27.9 %copy-start.9 = (f32[2,8,128,128]{3,2,1,0:T(8,128)S(1)}, f32[2,8,128,128]{3,2,1,0:T(8,128)}, u32[]{:S(2)}) copy-start(f32[2,8,128,128]{3,2,1,0:T(8,128)} %copy-done.8) | copy-start | bytes 3145732
  705.3 9.9 copy-start.27
  705.3 128.4 %reduce-scatter.13.cloned.1.call-start = ((), (), s32[]{:S(2)}) async-start(), calls=%async_computation.7 | async-start | bytes 9437184
  705.3 9.9 copy-start.31
  705.3 9.9 copy-start.32
  713.2 1.3 copy-start.28
  713.2 2.0 copy-start.29
  753.3 161.2 %reduce-scatter.17.cloned.1.call-start = ((), (), s32[]{:S(2)}) async-start(), calls=%async_computation.9 | async-start | bytes 12976128
  813.6 1.6 copy-start.34
  813.6 163.4 %reduce-scatter.11.cloned.1.call-start = ((), (), s32[]{:S(2)}) async-start(), calls=%async_computation.4 | async-start | bytes 6488064 | tf_op jit(solution)/shard_map/reduce_scatter | solution.py:175
  831.2 281.9 %all-reduce.3.cloned.1.call-start = ((), (), s32[]{:S(2)}) async-start(), calls=%async_computation.10 | async-start | bytes 6946816 | tf_op jit(solution)/shard_map/psum | solution.py:182
  837.4 139.5 %copy-start.11 = (bf16[2,512,1024]{2,1,0:T(8,128)(2,1)S(1)}, bf16[2,512,1024]{2,1,0:T(8,128)(2,1)}, u32[]{:S(2)}) copy-start(bf16[2,512,1024]{2,1,0:T(8,128)(2,1)} %param.11) | copy-start | bytes 6291460
  977.0 14.4 %copy-start.4 = (f32[1024,1024]{1,0:T(8,128)S(1)}, f32[1024,1024]{1,0:T(8,128)}, u32[]{:S(2)}) copy-start(f32[1024,1024]{1,0:T(8,128)} %copy-done.2) | copy-start | bytes 12582916
  991.4 3.5 copy-start.13
  1114.5 5.1 copy-start.35
  (2 other events, 1.7 us)
Sparse Core Ops, SparseCore 0:
  10.5 91.6 all-gather.4
  131.7 58.1 all-gather.6
  705.4 40.7 reduce-scatter.14
  753.4 70.9 reduce-scatter.12
  827.7 86.7 reduce-scatter.16
  917.9 59.0 reduce-scatter.10
  980.3 132.6 all-reduce.2
